TPU v7x, 32 devices: a whole 2x2x4 slice. The times are simulated.
32 devices in a mesh: row: 8 (over z, y), col: 2 (over core), layer: 2 (over x).
Axes of the slice: x: 2, y: 2, z: 4, core: 2. Of those that a mesh axis runs over, the one named last changes fastest.
Arguments:
- matrix: float32 [1, 8, 256, 4, 2, 256], P(None, 'row', None, None, 'col'), may hold values from -8 to 113.137085, as said below
Outputs:
- factored: float32 [1, 8, 256, 4, 2, 256], P(None, 'row', None, 'layer', 'col')
Inputs may be any that keep to these rules, and one draw needn't show every extreme that they name: `matrix`: viewed as in the first step it is symmetric, its leading 2 * 256 x 2 * 256 block is positive definite, and its diagonal entries lie between 2.5 and 5 times the square root of 512.
All inputs are finite; a program needn't handle non-finite values.
Results may differ from a plain program's by a relative error of at most 0.000059.
Values sent between devices are 32-bit elements; how exact they have to be, the bound alone decides.
No kernel may reach another device: no remote copies, remote signals or barrier semaphores. Data moves between devices by JAX's collectives and lax.ppermute only.
A program may use at most 128 MiB of HBM per device.

v0:
```python
import jax
import jax.numpy as jnp
from jax import lax
from jax.sharding import PartitionSpec as P

HIGH = lax.Precision.HIGHEST


def from_root(shard, axis, root):
    mine = lax.axis_index(axis) == root
    return lax.psum(jnp.where(mine, shard, jnp.zeros_like(shard)), axis)


def factor_block(diag_block):
    lower_fac = jnp.linalg.cholesky(diag_block)
    identity = jnp.eye(diag_block.shape[0], dtype=jnp.float32)
    inverse = lax.linalg.triangular_solve(lower_fac, identity, left_side=True, lower=True)
    return (lower_fac, inverse)


def on_device(matrix):
    row_total = lax.axis_size("row")
    col_total = lax.axis_size("col")
    layer_total = lax.axis_size("layer")
    grid_row = lax.axis_index("row")
    grid_col = lax.axis_index("col")
    grid_layer = lax.axis_index("layer")
    row_blocks = matrix.shape[0]
    block_size = matrix.shape[2]
    col_blocks = matrix.shape[3]
    half = block_size // layer_total
    owned = col_blocks // layer_total
    rows = row_blocks * block_size
    tile = matrix.reshape(rows, col_blocks * block_size)
    row_ids = jnp.arange(rows) // block_size * row_total + grid_row
    column = tile[:, :block_size]
    pending = None
    total = None
    panels = []
    for section in range(2):
        diag_block = from_root(column, "row", section % row_total)
        lower_fac, inverse = factor_block(diag_block)
        solved = jnp.dot(column, inverse.T, precision=HIGH, preferred_element_type=jnp.float32)
        repeated = jnp.tile(lower_fac, (row_blocks, 1))
        complete = jnp.where(
            row_ids[:, None] > section,
            solved,
            jnp.where(row_ids[:, None] == section, repeated, 0.0),
        )
        panels.append(complete)
        share = lax.dynamic_slice_in_dim(complete, grid_layer * half, half, 1)
        share = from_root(share, "col", section % col_total)
        gathered = lax.all_gather(
            share.reshape(row_blocks, 1, block_size, half), "row", axis=1, tiled=True
        )
        grouped = gathered.reshape(col_blocks, col_total, block_size, half)
        picked = lax.dynamic_index_in_dim(grouped, grid_col, 1, keepdims=False).reshape(
            col_blocks * block_size, half
        )
        update = lax.dot_general(
            share,
            picked,
            (((1,), (1,)), ((), ())),
            precision=HIGH,
            preferred_element_type=jnp.float32,
        )
        if section == 0:
            head = lax.psum(update[:, :block_size], "layer")
            column = tile[:, :block_size] - head
            pending = update
        else:
            total = pending + update
    reduced = lax.psum_scatter(
        total.reshape(rows, col_blocks, block_size), "layer", scatter_dimension=1, tiled=True
    )
    own_part = (
        lax.dynamic_slice_in_dim(
            tile.reshape(rows, col_blocks, block_size), grid_layer * owned, owned, 1
        )
        - reduced
    )
    replacement = jnp.where(grid_col == 0, panels[0], panels[1])
    global_ids = (grid_layer * owned + jnp.arange(owned)) * col_total + grid_col
    result = jnp.where((global_ids < 2)[None, :, None], replacement[:, None, :], own_part)
    return result.reshape(row_blocks, 1, block_size, owned, 1, block_size)


def solution(mesh):
    in_specs = (P(None, "row", None, None, "col", None),)
    out_specs = P(None, "row", None, "layer", "col", None)
    return jax.shard_map(
        on_device, mesh=mesh, in_specs=in_specs, out_specs=out_specs, check_vma=False
    )
```

profile of v0, /device:TPU:0, one launch (start us, length us, event | category | flops | bytes accessed | tf_op | source)
XLA Modules:
  0.0 472.5 jit_solution(6674159370767984335)
XLA Ops:
  6.5 2.3 copy.16
  9.8 74.7 %all-reduce.7.cloned.1.call-done = f32[256,256]{0,1:T(8,128)} async-done(((f32[256,256]{0,1:T(8,128)}), f32[256,256]{0,1:T(8,128)}) %all-reduce.7.cloned.1.call-update) | async-done | bytes 262160 | tf_op jit(solution)/shard_map/psum | solution.py:11
  85.7 11.7 %cholesky.130 = f32[128,128]{1,0:T(8,128)S(1)} custom-call(f32[128,128]{1,0:T(8,128)S(1)} %cholesky.194), custom_call_target="Cholesky" | custom-call | tf_op jit(solution)/shard_map/jit(cholesky)/cholesky | solution.py:15
  97.4 9.8 %custom-call.13 = f32[1,128,128]{1,2,0:T(8,128)S(1)} custom-call(f32[1,128,128]{2,1,0:T(8,128)S(1)} %get-tuple-element.62), custom_call_target="InvertDiagBlocksLowerTriangular" | custom-call | tf_op jit(solution)/shard_map/jit(cholesky)/cholesky | solution.py:15
  107.7 11.7 %cholesky.147 = f32[128,128]{1,0:T(8,128)S(1)} custom-call(f32[128,128]{1,0:T(8,128)S(1)} %convolution_subtract_fusion.3), custom_call_target="Cholesky" | custom-call | tf_op jit(solution)/shard_map/jit(cholesky)/cholesky | solution.py:15
  122.0 4.8 %while.4 = (s32[]{:T(128)}, f32[256,256]{0,1:T(8,128)S(1)}, s32[2,2]{1,0:T(2,128)S(1)}, f32[2,128,128]{2,1,0:T(8,128)S(1)}, s32[]{:T(128)}) while((s32[]{:T(128)}, f32[256,256]{0,1:T(8,128)S(1)}, s32[2,2]{1,0:T(2,128)S(1)}, f32[2,128,128]{2,1,0:T(8,128)S(1)}, s32[]{:T(128)}) %tuple.46), condition=%wide.while_cond, body=%wide.while_body.sunk | while | flops 2 | bytes 393321 | solution.py:17
  126.8 19.7 %custom-call.14 = f32[2,128,128]{1,2,0:T(8,128)S(1)} custom-call(f32[2,128,128]{2,1,0:T(8,128)S(1)} %get-tuple-element.21), custom_call_target="InvertDiagBlocksLowerTriangular" | custom-call | tf_op jit(solution)/shard_map/triangular_solve/custom-call.0 | solution.py:17
  148.6 17.2 %all-reduce.9.cloned.1.call-done = f32[256,128]{0,1:T(8,128)} async-done(((f32[256,128]{0,1:T(8,128)}), f32[256,128]{0,1:T(8,128)}) %all-reduce.9.cloned.1.call-update) | async-done | bytes 131088 | tf_op jit(solution)/shard_map/psum | solution.py:11
  165.9 42.6 %all-gather.5.cloned.1.call-done = f32[2048,128]{0,1:T(8,128)} async-done(((f32[256,128]{0,1:T(8,128)}), f32[2048,128]{0,1:T(8,128)}) %all-gather.5.cloned.1.call-update) | async-done | bytes 1048592 | tf_op jit(solution)/shard_map/all_gather | solution.py:53
  208.5 2.1 reshape.86
  210.6 1.6 dynamic-slice_reduce_fusion.1
  215.1 22.4 %all-reduce.11.cloned.1.call-done = f32[256,256]{0,1:T(8,128)} async-done(((f32[256,256]{0,1:T(8,128)}), f32[256,256]{0,1:T(8,128)}) %all-reduce.11.cloned.1.call-update) | async-done | bytes 262160 | tf_op jit(solution)/shard_map/psum | solution.py:68
  237.5 1.7 broadcast_select_fusion
  239.5 72.3 %all-reduce.13.cloned.1.call-done = f32[256,256]{0,1:T(8,128)} async-done(((f32[256,256]{0,1:T(8,128)}), f32[256,256]{0,1:T(8,128)}) %all-reduce.13.cloned.1.call-update) | async-done | bytes 262160 | tf_op jit(solution)/shard_map/psum | solution.py:11
  313.0 11.7 %cholesky.164 = f32[128,128]{1,0:T(8,128)S(1)} custom-call(f32[128,128]{1,0:T(8,128)S(1)} %cholesky.197), custom_call_target="Cholesky" | custom-call | tf_op jit(solution)/shard_map/jit(cholesky)/cholesky | solution.py:15
  324.8 9.8 %custom-call.15 = f32[1,128,128]{1,2,0:T(8,128)S(1)} custom-call(f32[1,128,128]{2,1,0:T(8,128)S(1)} %get-tuple-element.60), custom_call_target="InvertDiagBlocksLowerTriangular" | custom-call | tf_op jit(solution)/shard_map/jit(cholesky)/cholesky | solution.py:15
  335.1 11.7 %cholesky.181 = f32[128,128]{1,0:T(8,128)S(1)} custom-call(f32[128,128]{1,0:T(8,128)S(1)} %convolution_subtract_fusion.2), custom_call_target="Cholesky" | custom-call | tf_op jit(solution)/shard_map/jit(cholesky)/cholesky | solution.py:15
  349.8 4.4 while.5
  354.2 19.7 %custom-call.16 = f32[2,128,128]{1,2,0:T(8,128)S(1)} custom-call(f32[2,128,128]{2,1,0:T(8,128)S(1)} %get-tuple-element.22), custom_call_target="InvertDiagBlocksLowerTriangular" | custom-call | tf_op jit(solution)/shard_map/triangular_solve/custom-call.0 | solution.py:17
  376.7 17.2 %all-reduce.15.cloned.1.call-done = f32[256,128]{0,1:T(8,128)} async-done(((f32[256,128]{0,1:T(8,128)}), f32[256,128]{0,1:T(8,128)}) %all-reduce.15.cloned.1.call-update) | async-done | bytes 131088 | tf_op jit(solution)/shard_map/psum | solution.py:11
  393.9 42.6 %all-gather.7.cloned.1.call-done = f32[2048,128]{0,1:T(8,128)} async-done(((f32[256,128]{0,1:T(8,128)}), f32[2048,128]{0,1:T(8,128)}) %all-gather.7.cloned.1.call-update) | async-done | bytes 1048592 | tf_op jit(solution)/shard_map/all_gather | solution.py:53
  436.6 2.1 reshape.89
  438.7 1.6 dynamic-slice_reduce_fusion
  445.0 17.9 %reduce-scatter.2.cloned.1.call-done = f32[256,2,256]{2,0,1:T(8,128)} async-done(((f32[256,4,256]{2,0,1:T(8,128)}), f32[256,2,256]{2,0,1:T(8,128)}) %reduce-scatter.2.cloned.1.call-update) | async-done | bytes 524304 | tf_op jit(solution)/shard_map/reduce_scatter | solution.py:73
  (109 shorter events, 30.6 us)
Async XLA Ops:
  6.5 77.9 %all-reduce.7.cloned.1.call-start = ((), (), s32[]{:S(2)}) async-start(), calls=%async_computation.1 | async-start | bytes 524288 | tf_op jit(solution)/shard_map/psum | solution.py:11
  9.6 156.2 %all-reduce.9.cloned.1.call-start = ((), (), s32[]{:S(2)}) async-start(), calls=%async_computation.2 | async-start | bytes 262144 | tf_op jit(solution)/shard_map/psum | solution.py:11
  84.4 1.2 copy-start.1
  148.5 60.0 %all-gather.5.cloned.1.call-start = ((), (), s32[]{:S(2)}) async-start(), calls=%async_computation.7 | async-start | bytes 1179648 | tf_op jit(solution)/shard_map/all_gather | solution.py:53
  165.8 71.7 %all-reduce.11.cloned.1.call-start = ((), (), s32[]{:S(2)}) async-start(), calls=%async_computation.3 | async-start | bytes 524288 | tf_op jit(solution)/shard_map/psum | solution.py:68
  212.2 0.9 copy-start.4
  215.0 96.7 %all-reduce.13.cloned.1.call-start = ((), (), s32[]{:S(2)}) async-start(), calls=%async_computation.4 | async-start | bytes 524288 | tf_op jit(solution)/shard_map/psum | solution.py:11
  239.2 154.7 %all-reduce.15.cloned.1.call-start = ((), (), s32[]{:S(2)}) async-start(), calls=%async_computation.5 | async-start | bytes 262144 | tf_op jit(solution)/shard_map/psum | solution.py:11
  311.8 1.2 copy-start.2
  374.6 1.0 copy-start.3
  376.6 59.9 %all-gather.7.cloned.1.call-start = ((), (), s32[]{:S(2)}) async-start(), calls=%async_computation.8 | async-start | bytes 1179648 | tf_op jit(solution)/shard_map/all_gather | solution.py:53
  393.9 69.0 %reduce-scatter.2.cloned.1.call-start = ((), (), s32[]{:S(2)}) async-start(), calls=%async_computation.6 | async-start | bytes 1572864 | tf_op jit(solution)/shard_map/reduce_scatter | solution.py:73
  440.3 0.9 copy-start.5
  443.3 1.2 copy-start
Sparse Core Ops, SparseCore 0:
  10.7 73.7 all-reduce.6
  148.7 17.0 all-reduce.8
  167.8 40.5 all-gather.4
  215.2 22.2 all-reduce.10
  240.7 71.0 all-reduce.12
  376.7 17.0 all-reduce.14
  395.9 40.5 all-gather.6
  443.5 19.3 reduce-scatter.1
where the time goes:
time: 481 us; the launch traced here: 472 us
  waiting for transfers between devices  307 us (64%)
  other arithmetic  113 us (23%)
  local copies, waits for them, and re-layouts  28.5 us (6%)
  between operations  16.8 us (3%)
  matrix products  5.65 us (1%)
    psum x4, waiting for transfers between devices, from_root(): return lax.psum(jnp.where(mine, shard, jnp.zeros_like(shard)), axis)  181 us
    all_gather x2, waiting for transfers between devices, on_device(): lax.all_gather(share.reshape(row_blocks, 1, block_size, half), 'row', axi...  85.2 us
    another operation x13, other arithmetic, factor_block(): lower_fac = jnp.linalg.cholesky(diag_block)  68.7 us
    another operation x5, other arithmetic, factor_block(): lax.linalg.triangular_solve(lower_fac, identity, left_side=True, lower=True)  39.4 us
    psum x1, waiting for transfers between devices, on_device(): head = lax.psum(update[:, :block_size], 'layer')  22.4 us
    reduce_scatter x1, waiting for transfers between devices, on_device(): lax.psum_scatter(total.reshape(rows, col_blocks, block_size), 'layer', sc...  17.9 us
  transfers between devices with their start and end apart: 8, of which 8 were waited for; matrix products, arithmetic and copies ran while one was open for 0% of the time, Pallas kernels for 0%

commit v1 on v0

--- a/solution.py
+++ b/solution.py
@@ -8,7 +8,13 @@
 
 def from_root(shard, axis, root):
     mine = lax.axis_index(axis) == root
-    return lax.psum(jnp.where(mine, shard, jnp.zeros_like(shard)), axis)
+
+    def _point_spans(x_part, bus_axis):
+        far_arr = lax.all_gather(x_part, axis_name=bus_axis)
+        main = jnp.sum(far_arr, axis=0)
+        return main
+
+    return _point_spans(jnp.where(mine, shard, jnp.zeros_like(shard)), axis)
 
 
 def factor_block(diag_block):

time: 481 us -> 386 us (0.80); the launches traced: 472 us -> 385 us
  waiting for transfers between devices: 307 us -> 219 us
  local copies, waits for them, and re-layouts: 28.5 us -> 15.5 us
  other arithmetic: 113 us -> 121 us
    psum x4 -> x0, waiting for transfers between devices: 181 us -> none  [from_root(): return lax.psum(jnp.where(mine, shard, jnp.zeros_like(shard)), axis)]
    all_gather x0 -> x2, waiting for transfers between devices: none -> 101 us  [_point_spans(): far_arr = lax.all_gather(x_part, axis_name=bus_axis)]
    all_gather x2, waiting for transfers between devices: 85.2 us -> 77.8 us  [on_device(): lax.all_gather(share.reshape(row_blocks, 1, block_size, half), 'row', axi...]
    unnamed x16 -> x7, local copies, waits for them, and re-layouts: 6.78 us -> 1.32 us
    reduce_sum x0 -> x4, other arithmetic: none -> 4.85 us  [_point_spans(): main = jnp.sum(far_arr, axis=0)]
  transfers between devices with their start and end apart: 8 -> 6, of which waited for: 8 -> 6; matrix products, arithmetic and copies ran while one was open for 0% -> 0% of each run, Pallas kernels for 0% -> 0%
where the time goes in v1:
time: 386 us; the launch traced here: 385 us
  waiting for transfers between devices  219 us (57%)
  other arithmetic  121 us (31%)
  between operations  16.5 us (4%)
  local copies, waits for them, and re-layouts  15.5 us (4%)
  matrix products  7.36 us (2%)
  blocking collectives  3.99 us (1%)
    all_gather x2, waiting for transfers between devices, _point_spans(): far_arr = lax.all_gather(x_part, axis_name=bus_axis)  101 us
    all_gather x2, waiting for transfers between devices, on_device(): lax.all_gather(share.reshape(row_blocks, 1, block_size, half), 'row', axi...  77.8 us
    another operation x13, other arithmetic, factor_block(): lower_fac = jnp.linalg.cholesky(diag_block)  68.7 us
    another operation x5, other arithmetic, factor_block(): lax.linalg.triangular_solve(lower_fac, identity, left_side=True, lower=True)  40.2 us
    psum x1, waiting for transfers between devices, on_device(): head = lax.psum(update[:, :block_size], 'layer')  22.1 us
    reduce_scatter x1, waiting for transfers between devices, on_device(): lax.psum_scatter(total.reshape(rows, col_blocks, block_size), 'layer', sc...  18.4 us
    another operation x15, local copies, waits for them, and re-layouts, factor_block(): lax.linalg.triangular_solve(lower_fac, identity, left_side=True, lower=True)  8.21 us
  transfers between devices with their start and end apart: 6, of which 6 were waited for; matrix products, arithmetic and copies ran while one was open for 0% of the time, Pallas kernels for 0%

profile of v1, /device:TPU:0, one launch (start us, length us, event | category | flops | bytes accessed | tf_op | source)
XLA Modules:
  0.0 385.2 jit_solution(5795658071021773019)
XLA Ops:
  6.5 4.0 %reduce.8 = f32[256,4,256]{2,1,0:T(4,128)S(1)} reduce(f32[1,1,256,4,1,256]{5,4,3,2,1,0:T(1,128)} %param.4, f32[]{:T(128)} %constant.138), dimensions={0,1,4}, to_apply=%param.4.reduce_sub_computation | reduce | bytes 2097156 | tf_op args[0]
  11.8 51.7 %all-gather.11.cloned.1.call-done = f32[2048,256]{1,0:T(8,128)} async-done(((f32[256,256]{1,0:T(8,128)}), f32[2048,256]{1,0:T(8,128)}) %all-gather.11.cloned.1.call-update) | async-done | bytes 2097168 | tf_op jit(solution)/shard_map/all_gather | solution.py:13
  63.4 1.8 reduce_sum.36
  65.4 11.7 %cholesky.130 = f32[128,128]{1,0:T(8,128)S(1)} custom-call(f32[128,128]{1,0:T(8,128)S(1)} %cholesky.194), custom_call_target="Cholesky" | custom-call | tf_op jit(solution)/shard_map/jit(cholesky)/cholesky | solution.py:21
  77.1 9.8 %custom-call.13 = f32[1,128,128]{1,2,0:T(8,128)S(1)} custom-call(f32[1,128,128]{2,1,0:T(8,128)S(1)} %get-tuple-element.50), custom_call_target="InvertDiagBlocksLowerTriangular" | custom-call | tf_op jit(solution)/shard_map/jit(cholesky)/cholesky | solution.py:21
  87.5 11.7 %cholesky.147 = f32[128,128]{1,0:T(8,128)S(1)} custom-call(f32[128,128]{1,0:T(8,128)S(1)} %convolution_subtract_fusion.3), custom_call_target="Cholesky" | custom-call | tf_op jit(solution)/shard_map/jit(cholesky)/cholesky | solution.py:21
  101.4 4.3 %while.4 = (s32[]{:T(128)}, f32[256,256]{1,0:T(8,128)S(1)}, s32[2,2]{1,0:T(2,128)S(1)}, f32[2,128,128]{2,1,0:T(8,128)S(1)}, s32[]{:T(128)}) while((s32[]{:T(128)}, f32[256,256]{1,0:T(8,128)S(1)}, s32[2,2]{1,0:T(2,128)S(1)}, f32[2,128,128]{2,1,0:T(8,128)S(1)}, s32[]{:T(128)}) %tuple.46), condition=%wide.while_cond, body=%wide.while_body.sunk | while | flops 2 | bytes 131181 | solution.py:23
  105.7 19.7 %custom-call.14 = f32[2,128,128]{1,2,0:T(8,128)S(1)} custom-call(f32[2,128,128]{2,1,0:T(8,128)S(1)} %get-tuple-element.21), custom_call_target="InvertDiagBlocksLowerTriangular" | custom-call | tf_op jit(solution)/shard_map/triangular_solve/custom-call.0 | solution.py:23
  126.8 2.0 all-gather.1
  129.5 38.9 %all-gather.13.cloned.1.call-done = f32[2048,128]{1,0:T(8,128)} async-done(((f32[256,128]{1,0:T(8,128)}), f32[2048,128]{1,0:T(8,128)}) %all-gather.13.cloned.1.call-update) | async-done | bytes 1048592 | tf_op jit(solution)/shard_map/all_gather | solution.py:59
  169.5 1.9 fusion.36
  172.2 22.1 %all-reduce.3.cloned.1.call-done = f32[256,256]{1,0:T(8,128)} async-done(((f32[256,256]{1,0:T(8,128)}), f32[256,256]{1,0:T(8,128)}) %all-reduce.3.cloned.1.call-update) | async-done | bytes 262160 | tf_op jit(solution)/shard_map/psum | solution.py:74
  194.3 1.7 broadcast_select_fusion
  196.1 49.3 %all-gather.15.cloned.1.call-done = f32[2048,256]{1,0:T(8,128)} async-done(((f32[256,256]{1,0:T(8,128)}), f32[2048,256]{1,0:T(8,128)}) %all-gather.15.cloned.1.call-update) | async-done | bytes 2097168 | tf_op jit(solution)/shard_map/all_gather | solution.py:13
  245.4 1.8 reduce_sum.38
  247.4 11.7 %cholesky.164 = f32[128,128]{1,0:T(8,128)S(1)} custom-call(f32[128,128]{1,0:T(8,128)S(1)} %cholesky.197), custom_call_target="Cholesky" | custom-call | tf_op jit(solution)/shard_map/jit(cholesky)/cholesky | solution.py:21
  259.2 9.8 %custom-call.15 = f32[1,128,128]{1,2,0:T(8,128)S(1)} custom-call(f32[1,128,128]{2,1,0:T(8,128)S(1)} %get-tuple-element.46), custom_call_target="InvertDiagBlocksLowerTriangular" | custom-call | tf_op jit(solution)/shard_map/jit(cholesky)/cholesky | solution.py:21
  269.5 11.7 %cholesky.181 = f32[128,128]{1,0:T(8,128)S(1)} custom-call(f32[128,128]{1,0:T(8,128)S(1)} %convolution_subtract_fusion.2), custom_call_target="Cholesky" | custom-call | tf_op jit(solution)/shard_map/jit(cholesky)/cholesky | solution.py:21
  284.0 4.4 %while.5 = (s32[]{:T(128)}, f32[256,256]{1,0:T(8,128)S(1)}, s32[2,2]{1,0:T(2,128)S(1)}, f32[2,128,128]{2,1,0:T(8,128)S(1)}, s32[]{:T(128)}) while((s32[]{:T(128)}, f32[256,256]{1,0:T(8,128)S(1)}, s32[2,2]{1,0:T(2,128)S(1)}, f32[2,128,128]{2,1,0:T(8,128)S(1)}, s32[]{:T(128)}) %tuple.64), condition=%wide.while_cond.clone, body=%wide.while_body.clone.sunk | while | flops 2 | bytes 131181 | solution.py:23
  289.0 20.5 %custom-call.16 = f32[2,128,128]{1,2,0:T(8,128)S(1)} custom-call(f32[2,128,128]{2,1,0:T(8,128)} %copy-done.2), custom_call_target="InvertDiagBlocksLowerTriangular" | custom-call | tf_op jit(solution)/shard_map/triangular_solve/custom-call.0 | solution.py:23
  310.9 2.0 all-gather.4
  313.6 38.9 %all-gather.17.cloned.1.call-done = f32[2048,128]{1,0:T(8,128)} async-done(((f32[256,128]{1,0:T(8,128)}), f32[2048,128]{1,0:T(8,128)}) %all-gather.17.cloned.1.call-update) | async-done | bytes 1048592 | tf_op jit(solution)/shard_map/all_gather | solution.py:59
  353.6 1.9 convolution_add_fusion
  357.5 18.4 %reduce-scatter.2.cloned.1.call-done = f32[256,2,256]{2,0,1:T(8,128)} async-done(((f32[256,4,256]{2,0,1:T(8,128)}), f32[256,2,256]{2,0,1:T(8,128)}) %reduce-scatter.2.cloned.1.call-update) | async-done | bytes 524304 | tf_op jit(solution)/shard_map/reduce_scatter | solution.py:79
  (80 shorter events, 25.2 us)
Async XLA Ops:
  6.5 56.9 %all-gather.11.cloned.1.call-start = ((), (), s32[]{:S(2)}) async-start(), calls=%async_computation.3 | async-start | bytes 2359296 | tf_op jit(solution)/shard_map/all_gather | solution.py:13
  11.5 157.0 %all-gather.13.cloned.1.call-start = ((), (), s32[]{:S(2)}) async-start(), calls=%async_computation.4 | async-start | bytes 1179648 | tf_op jit(solution)/shard_map/all_gather | solution.py:59
  129.5 64.8 %all-reduce.3.cloned.1.call-start = ((), (), s32[]{:S(2)}) async-start(), calls=%async_computation.1 | async-start | bytes 524288 | tf_op jit(solution)/shard_map/psum | solution.py:74
  172.2 73.3 %all-gather.15.cloned.1.call-start = ((), (), s32[]{:S(2)}) async-start(), calls=%async_computation.5 | async-start | bytes 2359296 | tf_op jit(solution)/shard_map/all_gather | solution.py:13
  196.0 156.5 %all-gather.17.cloned.1.call-start = ((), (), s32[]{:S(2)}) async-start(), calls=%async_computation.6 | async-start | bytes 1179648 | tf_op jit(solution)/shard_map/all_gather | solution.py:59
  247.4 63.0 %copy-start.1 = (f32[256,256]{1,0:T(8,128)S(1)}, f32[256,256]{1,0:T(8,128)}, u32[]{:S(2)}) copy-start(f32[256,256]{1,0:T(8,128)} %all-reduce.3.cloned.1.call-done) | copy-start | bytes 786436
  288.3 0.7 copy-start.2
  313.6 62.3 %reduce-scatter.2.cloned.1.call-start = ((), (), s32[]{:S(2)}) async-start(), calls=%async_computation.2 | async-start | bytes 1572864 | tf_op jit(solution)/shard_map/reduce_scatter | solution.py:79
  355.5 1.6 copy-start
Sparse Core Ops, SparseCore 0:
  11.6 51.8 all-gather.10
  129.6 38.7 all-gather.12
  172.3 21.9 all-reduce.2
  196.3 49.0 all-gather.14
  313.7 38.7 all-gather.16
  356.8 19.0 reduce-scatter.1
